TPU v7x, 32 devices: a whole 2x2x4 slice. The times are simulated.
32 devices in a mesh: space: 8 (over y, x, core), tm: 4 (over z).
Axes of the slice: x: 2, y: 2, z: 4, core: 2. Of those that a mesh axis runs over, the one named last changes fastest.
Arguments:
- series: bfloat16 [16384, 2, 512], P('space', None, 'tm'), may hold values from -6 to 6
- space_basis: bfloat16 [16384, 16384], P('space', 'tm'), may hold values from -0.046875 to 0.046875
- time_basis: bfloat16 [512, 512], P('tm'), may hold values from -0.25 to 0.25
- space_eig: float32 [16384], replicated, may hold values from 0.3 to 3
- time_eig: float32 [512], replicated, may hold values from 0.3 to 3
Outputs:
- alpha: bfloat16 [16384, 2, 512], P('space', None, 'tm')
- grad_space: bfloat16 [16384, 8, 2048], P('space', None, 'tm')
All inputs are finite; a program needn't handle non-finite values.
Results may differ from a plain program's by a relative error of at most 0.0063.
Values may be sent and summed in bfloat16 or wider, within the bound.
A program may use at most 128 MiB of HBM per device.

v0:
```python
import functools

import jax
import jax.numpy as jnp
from jax import lax
from jax.experimental import pallas as pl
from jax.experimental.pallas import tpu as pltpu
from jax.sharding import PartitionSpec as P

F32 = jnp.float32
BF16 = jnp.bfloat16
MESH = pl.DeviceIdType.MESH
CONTRACT_LAST = (((1,), (1,)), ((), ()))
CONTRACT_FIRST = (((0,), (0,)), ((), ()))
VMEM_BYTES = 67043328
RING = 4
PIECES = 2


def rcopy(src, dst, send_sem, recv_sem, **where):
    return pltpu.make_async_remote_copy(
        src_ref=src,
        dst_ref=dst,
        send_sem=send_sem,
        recv_sem=recv_sem,
        device_id=where,
        device_id_type=MESH,
    )


def field_kernel(
    space_count,
    time_count,
    series_hbm, basis_hbm, tbasis_hbm, time_eig_ref, space_eig_ref,
    rows_hbm, cols_hbm,
    basis, series, tbasis, pair_out, pair_in, chip_out, chip_in, mine, scaled, partial, below, above, up_out, down_out,
    load_sem, xs_sem, xr_sem, ts_sem, tr_sem, ps_sem, pr_sem, cs_sem, cr_sem, gs_sem, gr_sem, fs_sem,
    us_sem, ur_sem, ds_sem, dr_sem, os_sem, ks_sem, kr_sem, kf_sem, ko_sem,
):
    reps, _, time_local, _ = series.shape
    _, blocks, block_rows, times = partial.shape
    own = mine.shape[1]
    pairs = space_count // 2
    last = time_count - 1
    sub_rows = blocks * block_rows // time_count
    me = lax.axis_index("space")
    z = lax.axis_index("tm")
    core = lax.rem(me, 2)
    chip = lax.div(me, 2)
    partner = me + 1 - 2 * core
    total = reps * blocks

    def chip_at(d):
        return lax.bitwise_xor(chip, d)

    def peer(d):
        return 2 * chip_at(d) + core

    barrier = pltpu.get_barrier_semaphore()

    def greet(**where):
        pl.semaphore_signal(barrier, inc=1, device_id=where, device_id_type=MESH)

    @pl.when(z > 0)
    def _():
        greet(tm=z - 1)

    @pl.when(z < last)
    def _():
        greet(tm=z + 1)

    greet(space=partner)
    for d in range(1, pairs):
        greet(space=peer(d))

    load_basis = pltpu.make_async_copy(basis_hbm, basis, load_sem.at[0])
    load_basis.start()
    load_tbasis = pltpu.make_async_copy(tbasis_hbm, tbasis.at[z], load_sem.at[1])
    load_tbasis.start()
    loads = [pltpu.make_async_copy(series_hbm.at[q], series.at[q, z], load_sem.at[2 + q]) for q in range(reps)]
    for load in loads:
        load.start()

    @pl.when(z == 0)
    def _():
        below[...] = jnp.zeros_like(below)

    @pl.when(z == last)
    def _():
        above[...] = jnp.zeros_like(above)

    pl.semaphore_wait(barrier, pairs + jnp.minimum(z, 1) + jnp.minimum(last - z, 1))

    def x_copy(q, j, way, step):
        return rcopy(series.at[q, j], series.at[q, j], xs_sem.at[q, way, step], xr_sem.at[q, j], tm=z + 1 - 2 * way)

    def t_copy(j, way, step):
        return rcopy(tbasis.at[j], tbasis.at[j], ts_sem.at[way, step], tr_sem.at[j], tm=z + 1 - 2 * way)

    def line_start(copy):
        @pl.when(z < last)
        def _():
            copy(z, 0, 0).start()

        @pl.when(z > 0)
        def _():
            copy(z, 1, 0).start()

    def line_step(copy, k):
        @pl.when(z >= k)
        def _():
            copy(z - k, 0, k).wait_recv()

            @pl.when(z < last)
            def _():
                copy(z - k, 0, k).start()

        @pl.when(z + k <= last)
        def _():
            copy(z + k, 1, k).wait_recv()

            @pl.when(z > 0)
            def _():
                copy(z + k, 1, k).start()

    def line_drain(copy):
        for k in range(time_count):
            @pl.when((z >= k) & (z < last))
            def _():
                copy(z - k, 0, k).wait_send()

            @pl.when((z + k <= last) & (z > 0))
            def _():
                copy(z + k, 1, k).wait_send()

    def x_of(q):
        return functools.partial(x_copy, q)

    def pair_copy(q, d):
        return rcopy(pair_out.at[d], pair_in.at[q, d], ps_sem.at[d], pr_sem.at[q, d], space=partner)

    def chip_copy(q, d):
        return rcopy(chip_out.at[d - 1], chip_in.at[q, d - 1], cs_sem.at[d - 1], cr_sem.at[q, d - 1], space=peer(d))

    def spectrum(q, j):
        flat = series[q].reshape(time_count * time_local, series.shape[3])
        return jnp.dot(flat, basis[:, pl.ds(pl.multiple_of(j * own, own), own)], preferred_element_type=F32)

    def spectral_pair(q):
        @pl.loop(0, pairs)
        def _(n):
            d = pairs - 1 - n
            if q > 0:
                pair_copy(q - 1, d).wait_send()
            pair_out[d] = spectrum(q, 2 * chip_at(d) + 1 - core).astype(BF16)
            pair_copy(q, d).start()

    def spectral_own(q):
        @pl.loop(0, pairs)
        def _(n):
            d = pairs - 1 - n
            value = spectrum(q, peer(d))
            pair_copy(q, d).wait_recv()
            value = value + pair_in[q, d].astype(F32)

            @pl.when(d > 0)
            def _():
                if q > 0:
                    chip_copy(q - 1, d).wait_send()
                chip_out[d - 1] = value.astype(BF16)
                chip_copy(q, d).start()

            @pl.when(d == 0)
            def _():
                mine[...] = value

    def gather_copy(q, d):
        at = pl.ds(pl.multiple_of(me * own, own), own)
        return rcopy(scaled.at[q, :, at], scaled.at[q, :, at], gs_sem.at[q, d - 1], gr_sem.at[q, me], space=peer(d))

    def forward_copy(q, j, d):
        at = pl.ds(pl.multiple_of(j * own, own), own)
        return rcopy(scaled.at[q, :, at], scaled.at[q, :, at], fs_sem.at[q, d], gr_sem.at[q, j], space=partner)

    def scale_own(q):
        value = mine[...]
        for d in range(1, pairs):
            chip_copy(q, d).wait_recv()
            value = value + chip_in[q, d - 1].astype(F32)
        rotation = tbasis[...].reshape(time_count * time_local, times)
        turned = lax.dot_general(rotation, value.astype(BF16), CONTRACT_FIRST, preferred_element_type=F32)
        turned = turned / (time_eig_ref[...] * space_eig_ref[...] + 0.1)
        scaled[q, :, pl.ds(pl.multiple_of(me * own, own), own)] = turned.astype(BF16)
        for d in reversed(range(1, pairs)):
            gather_copy(q, d).start()
        forward_copy(q, me, 0).start()

    def gather_forward(q):
        for d in range(1, pairs):
            forward_copy(q, peer(d), d).wait_recv()
            forward_copy(q, peer(d), d).start()

    def gather_finish(q):
        for d in range(pairs):
            forward_copy(q, peer(d) + 1 - 2 * core, d).wait_recv()

    def back(q, i):
        low = lax.div(i, 2)
        side = lax.rem(i, 2)
        side = jnp.where(2 * z < time_count, side, 1 - side)
        sub = jnp.where(side == 0, last - low, low)
        value = lax.dot_general(
            basis[pl.ds(pl.multiple_of(sub * sub_rows, sub_rows), sub_rows), :],
            scaled[q],
            CONTRACT_LAST,
            preferred_element_type=F32,
        )
        partial[q, pl.ds(sub * PIECES, PIECES)] = value.reshape(PIECES, block_rows, times)

    def up_copy(n, q, m):
        slot = lax.rem(n, RING)
        return rcopy(up_out.at[slot], below.at[q, m], us_sem.at[slot], ur_sem.at[n], tm=z + 1)

    def down_copy(n, q, m):
        slot = lax.rem(n, RING)
        return rcopy(down_out.at[slot], above.at[q, m], ds_sem.at[slot], dr_sem.at[n], tm=z - 1)

    def row_copy(q, m):
        return pltpu.make_async_copy(below.at[q, m], rows_hbm.at[q, m], os_sem.at[q * blocks + m])

    def finish_block(q, m):
        below[q, m] = (partial[q, m] + below[q, m].astype(F32) + above[q, m].astype(F32)).astype(BF16)
        row_copy(q, m).start()

    def up_step(n):
        at = n - z

        @pl.when((at >= 0) & (at < total))
        def _():
            q = lax.div(at, blocks)
            m = blocks - 1 - lax.rem(at, blocks)

            @pl.when(z > 0)
            def _():
                up_copy(at, q, m).wait_recv()

            @pl.when(z < last)
            def _():
                @pl.when(at >= RING)
                def _():
                    up_copy(at, q, m).wait_send()

                up_out[lax.rem(at, RING)] = (partial[q, m] + below[q, m].astype(F32)).astype(BF16)
                up_copy(at, q, m).start()

            @pl.when(q * blocks + m + last - z < n)
            def _():
                finish_block(q, m)

    def down_step(n):
        at = n - (last - z)

        @pl.when((at >= 0) & (at < total))
        def _():
            q = lax.div(at, blocks)
            m = lax.rem(at, blocks)

            @pl.when(z < last)
            def _():
                down_copy(at, q, m).wait_recv()

            @pl.when(z > 0)
            def _():
                @pl.when(at >= RING)
                def _():
                    down_copy(at, q, m).wait_send()

                down_out[lax.rem(at, RING)] = (partial[q, m] + above[q, m].astype(F32)).astype(BF16)
                down_copy(at, q, m).start()

            @pl.when(q * blocks + blocks - 1 - m + z <= n)
            def _():
                finish_block(q, m)

    def column_source(q):
        return below.at[q, pl.ds(z * PIECES, PIECES)]

    def column_copy(q, d):
        return rcopy(column_source(q), cols_hbm.at[q, me], ks_sem.at[q, d], kr_sem.at[q, me], space=peer(d))

    def column_pair(q):
        return rcopy(column_source(q), cols_hbm.at[q, me], kf_sem.at[q, 0], kr_sem.at[q, me], space=partner)

    def column_own(q):
        return pltpu.make_async_copy(column_source(q), cols_hbm.at[q, me], ko_sem.at[q])

    def column_forward(q, j, d):
        return rcopy(cols_hbm.at[q, j], cols_hbm.at[q, j], kf_sem.at[q, d], kr_sem.at[q, j], space=partner)

    def columns_start(q):
        for d in reversed(range(1, pairs)):
            column_copy(q, d).start()
        column_pair(q).start()
        column_own(q).start()

    def columns_relay(q):
        for d in range(1, pairs):
            column_forward(q, peer(d), d).wait_recv()
            column_forward(q, peer(d), d).start()

    def columns_finish(q):
        for d in range(pairs):
            column_forward(q, peer(d) + 1 - 2 * core, d).wait_recv()
        for d in range(1, pairs):
            column_copy(q, d).wait_send()
            column_forward(q, peer(d), d).wait_send()
        column_pair(q).wait_send()
        column_own(q).wait()

    for load in loads:
        load.wait()
    load_tbasis.wait()
    line_start(x_of(0))
    for k in range(1, time_count - 1):
        line_step(x_of(0), k)
    line_start(t_copy)
    for q in range(1, reps):
        line_start(x_of(q))
    for k in range(max(1, time_count - 1), time_count):
        line_step(x_of(0), k)
    line_step(t_copy, 1)
    load_basis.wait()
    for q in range(reps):
        if q > 0:
            for k in range(max(1, time_count - 1), time_count):
                line_step(x_of(q), k)
        spectral_pair(q)
        if q + 1 < reps:
            line_step(x_of(q + 1), 1)
        if q > 0:
            gather_forward(q - 1)
        spectral_own(q)
        if q + 1 < reps:
            for k in range(2, time_count - 1):
                line_step(x_of(q + 1), k)
            if q == 0:
                for k in range(2, time_count):
                    line_step(t_copy, k)
            scale_own(q)

    ahead = blocks // 2

    @pl.loop(0, total + last)
    def _(n):
        q = lax.div(n, blocks)
        i = lax.rem(n, blocks)

        @pl.when((q < reps) & (i < time_count))
        def _():
            @pl.when(i == 0)
            def _():
                @pl.when(q == reps - 1)
                def _():
                    gather_forward(reps - 1)

                gather_finish(q)

            back(q, i)

        up_step(n)
        down_step(n)
        for r in range(reps):
            low = z * PIECES
            ready = r * blocks + jnp.maximum(blocks - 1 - low + z, low + PIECES - 1 + last - z)

            @pl.when(n == ready)
            def _():
                columns_start(r)

        @pl.when(n == ahead)
        def _():
            scale_own(reps - 1)

        @pl.when(n == total - 1)
        def _():
            for r in range(reps - 1):
                columns_relay(r)

    columns_relay(reps - 1)
    for q in range(reps):
        columns_finish(q)
        line_drain(x_of(q))
        for d in range(1, pairs):
            gather_copy(q, d).wait_send()
        for d in range(pairs):
            forward_copy(q, peer(d), d).wait_send()
    line_drain(t_copy)
    for d in range(pairs):
        pair_copy(reps - 1, d).wait_send()
        if d > 0:
            chip_copy(reps - 1, d).wait_send()

    @pl.loop(0, total)
    def _(n):
        row_copy(lax.div(n, blocks), lax.rem(n, blocks)).wait()

    for n in range(total - min(RING, total), total):
        q, m = n // blocks, n % blocks

        @pl.when(z < last)
        def _():
            up_copy(n, q, m).wait_send()

        @pl.when(z > 0)
        def _():
            down_copy(n, q, m).wait_send()


def solve_field(series, basis, tbasis, time_eig, space_eig, space_count, time_count):
    reps, time_local, rows = series.shape
    depth = basis.shape[1]
    times = tbasis.shape[1]
    own = depth // space_count
    pairs = space_count // 2
    blocks = PIECES * time_count
    block_rows = rows // blocks
    dma = pltpu.SemaphoreType.DMA
    hbm = pl.BlockSpec(memory_space=pl.ANY)
    vmem = pl.BlockSpec(memory_space=pltpu.VMEM)
    return pl.pallas_call(
        functools.partial(field_kernel, space_count, time_count),
        out_shape=(
            jax.ShapeDtypeStruct((reps, blocks, block_rows, times), BF16),
            jax.ShapeDtypeStruct((reps, space_count, PIECES, block_rows, times), BF16),
        ),
        in_specs=[hbm, hbm, hbm, vmem, vmem],
        out_specs=(hbm, hbm),
        scratch_shapes=[
            pltpu.VMEM((rows, depth), BF16),
            pltpu.VMEM((reps, time_count, time_local, rows), BF16),
            pltpu.VMEM((time_count, time_local, times), BF16),
            pltpu.VMEM((pairs, times, own), BF16),
            pltpu.VMEM((reps, pairs, times, own), BF16),
            pltpu.VMEM((pairs - 1, times, own), BF16),
            pltpu.VMEM((reps, pairs - 1, times, own), BF16),
            pltpu.VMEM((times, own), F32),
            pltpu.VMEM((reps, times, depth), BF16),
            pltpu.VMEM((reps, blocks, block_rows, times), F32),
            pltpu.VMEM((reps, blocks, block_rows, times), BF16),
            pltpu.VMEM((reps, blocks, block_rows, times), BF16),
            pltpu.VMEM((RING, block_rows, times), BF16),
            pltpu.VMEM((RING, block_rows, times), BF16),
            dma((2 + reps,)),
            dma((reps, 2, time_count)),
            dma((reps, time_count)),
            dma((2, time_count)),
            dma((time_count,)),
            dma((pairs,)),
            dma((reps, pairs)),
            dma((pairs - 1,)),
            dma((reps, pairs - 1)),
            dma((reps, pairs - 1)),
            dma((reps, space_count)),
            dma((reps, pairs)),
            dma((RING,)),
            dma((reps * blocks,)),
            dma((RING,)),
            dma((reps * blocks,)),
            dma((reps * blocks,)),
            dma((reps, pairs)),
            dma((reps, space_count)),
            dma((reps, pairs)),
            dma((reps,)),
        ],
        compiler_params=pltpu.CompilerParams(
            collective_id=0, has_side_effects=True, vmem_limit_bytes=VMEM_BYTES
        ),
    )(series, basis, tbasis, time_eig, space_eig)


def grad_kernel(reps, scale, *refs):
    rows, columns = refs[:reps], refs[reps : 2 * reps]
    eig_ref, basis_ref, alpha_ref, grad_ref, alpha_scr, grad_scr, weighted_scr = refs[2 * reps :]
    tile, blocks, _ = grad_ref.shape
    for q in range(reps):
        block = rows[q][0]
        weighted_scr[q] = (block.astype(F32) * eig_ref[...] / scale).astype(BF16)
        alpha_scr[pl.ds(q, tile, stride=reps), :] = lax.dot_general(
            block, basis_ref[...], CONTRACT_LAST, preferred_element_type=F32
        )
    alpha_ref[...] = alpha_scr[...].astype(BF16).reshape(alpha_ref.shape)

    sub = columns[0].shape[2]
    @pl.loop(0, blocks)
    def _(a):
        total = None
        for q in range(reps):
            part = lax.dot_general(
                weighted_scr[q], columns[q][0, a], CONTRACT_LAST, preferred_element_type=F32
            )
            total = part if total is None else total + part
        for w in range(0, sub, 128):
            grad_scr[w // 128, pl.ds(a, tile, stride=blocks), :] = total[:, w : w + 128]
    for w in range(0, sub, 128):
        grad_ref[:, :, w : w + 128] = (
            grad_scr[w // 128].astype(BF16).reshape(tile, blocks, 128)
        )


def grad_and_alpha(rows, columns, time_eig, time_basis):
    reps, row_count, times = rows.shape
    _, blocks, sub, _ = columns.shape
    time_local = time_basis.shape[0]
    tile = min(row_count, 512)
    row_specs = [pl.BlockSpec((1, tile, times), lambda i, q=q: (q, i, 0)) for q in range(reps)]
    col_specs = [pl.BlockSpec((1, blocks, sub, times), lambda i, q=q: (q, 0, 0, 0)) for q in range(reps)]
    return pl.pallas_call(
        lambda *refs: grad_kernel(reps, reps * times, *refs),
        out_shape=(
            jax.ShapeDtypeStruct((row_count, reps, time_local), BF16),
            jax.ShapeDtypeStruct((row_count, blocks, sub), BF16),
        ),
        grid=(row_count // tile,),
        in_specs=row_specs
        + col_specs
        + [
            pl.BlockSpec((1, times), lambda i: (0, 0)),
            pl.BlockSpec((time_local, times), lambda i: (0, 0)),
        ],
        out_specs=(
            pl.BlockSpec((tile, reps, time_local), lambda i: (i, 0, 0)),
            pl.BlockSpec((tile, blocks, sub), lambda i: (i, 0, 0)),
        ),
        scratch_shapes=[
            pltpu.VMEM((tile * reps, time_local), F32),
            pltpu.VMEM((sub // 128, tile * blocks, 128), F32),
            pltpu.VMEM((reps, tile, times), BF16),
        ],
    )(*[rows] * reps, *[columns] * reps, time_eig[None, :], time_basis)


def per_device(series, space_basis, time_basis, space_eig, time_eig):
    space_count = lax.axis_size("space")
    time_count = lax.axis_size("tm")
    col_block = space_basis.shape[1]
    own = col_block // space_count
    first = lax.axis_index("tm") * col_block + lax.axis_index("space") * own
    space_own = lax.dynamic_slice_in_dim(space_eig, first, own)
    rows, columns = solve_field(
        jnp.transpose(series, (1, 2, 0)),
        space_basis,
        time_basis,
        time_eig[:, None],
        space_own[None, :],
        space_count,
        time_count,
    )
    reps, times = rows.shape[0], rows.shape[-1]
    return grad_and_alpha(
        rows.reshape(reps, -1, times), columns.reshape(reps, space_count, -1, times), time_eig, time_basis
    )


def solution(mesh):
    return jax.shard_map(
        per_device,
        mesh=mesh,
        in_specs=(P("space", None, "tm"), P("space", "tm"), P("tm", None), P(), P()),
        out_specs=(P("space", None, "tm"), P("space", None, "tm")),
        check_vma=False,
    )
```

profile of v0, /device:TPU:0, one launch (start us, length us, event | category | flops | bytes accessed | tf_op | source)
XLA Modules:
  0.0 302.5 jit_solution(18025906379181994785)
XLA Ops:
  0.6 1.4 dynamic_slice.3
  2.0 1.5 copy.9.time_eig_ref
  3.5 3.7 %copy.8 = bf16[2048,2,128]{0,2,1:T(8,128)(2,1)} copy(bf16[2048,2,128]{2,1,0:T(2,128)(2,1)} %param.5) | data formatting | bytes 2097152 | tf_op args[0]
  7.2 255.5 %shard_map.68 = (bf16[2,8,256,512]{3,2,1,0:T(8,128)(2,1)}, bf16[2,8,2,256,512]{4,3,2,1,0:T(8,128)(2,1)}) custom-call(bf16[2,128,2048]{2,1,0:T(8,128)(2,1)} %bitcast.10, bf16[2048,4096]{1,0:T(8,128)(2,1)} %basis_hbm.1, bf16[128,512]{1,0:T(8,128)(2,1)} %refs_5_.1, f32[512,1]{1,0:T(8,128)} %copy.9.time_eig_ref, f32[1,512]{1,0:T(1,128)} %bitcast.13), custom_call_target="tpu_custom_call" | custom-call | tf_op jit(solution)/shard_map/pallas_call | solution.py:430
  262.7 39.8 %shard_map.69 = (bf16[2048,2,128]{2,1,0:T(2,128)(2,1)}, bf16[2048,8,512]{2,1,0:T(8,128)(2,1)}) custom-call(bf16[2,2048,512]{2,1,0:T(8,128)(2,1)} %bitcast.8, bf16[2,2048,512]{2,1,0:T(8,128)(2,1)} %bitcast.9, bf16[2,8,512,512]{3,2,1,0:T(8,128)(2,1)} %bitcast.6, bf16[2,8,512,512]{3,2,1,0:T(8,128)(2,1)} %bitcast.7, f32[1,512]{1,0:T(1,128)} %bitcast.12, ...), custom_call_target="tpu_custom_call" | custom-call | tf_op jit(solution)/shard_map/pallas_call | solution.py:517
where the time goes:
time: 303 us; the launch traced here: 302 us
  Pallas kernels  295 us (97%)
  local copies, waits for them, and re-layouts  6.54 us (2%)
    pallas_call x1, Pallas kernels, solve_field(): pl.pallas_call(functools.partial(field_kernel, space_count, time_count),...  256 us
    pallas_call x1, Pallas kernels, grad_and_alpha(): pl.pallas_call(lambda *refs: grad_kernel(reps, reps * times, *refs), out_...  39.8 us

commit v1 on v0

v1 whole, which is shorter than its diff:
```python
import functools

import jax
import jax.numpy as jnp
from jax import lax
from jax.experimental import pallas as pl
from jax.experimental.pallas import tpu as pltpu
from jax.sharding import PartitionSpec as P

F32 = jnp.float32
BF16 = jnp.bfloat16
MESH = pl.DeviceIdType.MESH
CONTRACT_LAST = (((1,), (1,)), ((), ()))
CONTRACT_FIRST = (((0,), (0,)), ((), ()))
VMEM_BYTES = 67043328
RING = 4
PIECES = 4
PARTS = 2
LAG = 2


def rcopy(src, dst, send_sem, recv_sem, **where):
    return pltpu.make_async_remote_copy(
        src_ref=src,
        dst_ref=dst,
        send_sem=send_sem,
        recv_sem=recv_sem,
        device_id=where,
        device_id_type=MESH,
    )


def field_kernel(
    space_count,
    time_count,
    series_hbm, basis_hbm, tbasis_hbm, time_eig_ref, space_eig_ref,
    rows_hbm, cols_hbm,
    basis, series, tbasis, pair_out, pair_in, chip_out, chip_in, mine, scaled, partial, below, above, up_out, down_out,
    load_sem, xs_sem, xr_sem, ts_sem, tr_sem, te_sem, ps_sem, pr_sem, cs_sem, cr_sem, gs_sem, gr_sem, fs_sem,
    us_sem, ur_sem, ds_sem, dr_sem, os_sem, ks_sem, kr_sem, kf_sem, ko_sem,
):
    reps, _, time_local, _ = series.shape
    _, blocks, block_rows, times = partial.shape
    own = mine.shape[3]
    pairs = space_count // 2
    last = time_count - 1
    sub_rows = blocks * block_rows // time_count
    me = lax.axis_index("space")
    z = lax.axis_index("tm")
    core = lax.rem(me, 2)
    chip = lax.div(me, 2)
    partner = me + 1 - 2 * core
    total = reps * blocks

    def chip_at(d):
        return lax.bitwise_xor(chip, d)

    def peer(d):
        return 2 * chip_at(d) + core

    barrier = pltpu.get_barrier_semaphore()

    def greet(**where):
        pl.semaphore_signal(barrier, inc=1, device_id=where, device_id_type=MESH)

    @pl.when(z > 0)
    def _():
        greet(tm=z - 1)

    @pl.when(z < last)
    def _():
        greet(tm=z + 1)

    greet(space=partner)
    for d in range(1, pairs):
        greet(space=peer(d))

    loads = [pltpu.make_async_copy(series_hbm.at[q], series.at[q, z], load_sem.at[2 + q]) for q in range(reps)]
    for load in loads:
        load.start()
    share = time_local // pairs
    own_share = pl.ds(pl.multiple_of(chip * share, share), share)
    load_tbasis = pltpu.make_async_copy(tbasis_hbm.at[own_share], tbasis.at[z, own_share], load_sem.at[1])
    load_tbasis.start()
    load_basis = pltpu.make_async_copy(basis_hbm, basis, load_sem.at[0])

    @pl.when(z == 0)
    def _():
        below[...] = jnp.zeros_like(below)

    @pl.when(z == last)
    def _():
        above[...] = jnp.zeros_like(above)

    pl.semaphore_wait(barrier, pairs + jnp.minimum(z, 1) + jnp.minimum(last - z, 1))

    def x_copy(q, j, way, step, p):
        size = series.shape[3] // PARTS
        at = series.at[q, j, :, pl.ds(p * size, size)]
        return rcopy(at, at, xs_sem.at[q, way, step, p], xr_sem.at[q, j, p], tm=z + 1 - 2 * way)

    def t_copy(j, way, step, p):
        at = tbasis.at[j, own_share]
        return rcopy(at, at, ts_sem.at[way, step], tr_sem.at[j], tm=z + 1 - 2 * way)

    def t_share(d):
        at = tbasis.at[:, own_share]
        return rcopy(at, at, te_sem.at[0, d], te_sem.at[1, d], space=peer(d))

    def line_start(line):
        copy, parts = line
        for p in range(parts):
            @pl.when(z < last)
            def _():
                copy(z, 0, 0, p).start()

            @pl.when(z > 0)
            def _():
                copy(z, 1, 0, p).start()

    def line_part(line, k, p):
        copy, _ = line

        @pl.when(z >= k)
        def _():
            copy(z - k, 0, k, p).wait_recv()

            @pl.when(z < last)
            def _():
                copy(z - k, 0, k, p).start()

        @pl.when(z + k <= last)
        def _():
            copy(z + k, 1, k, p).wait_recv()

            @pl.when(z > 0)
            def _():
                copy(z + k, 1, k, p).start()

    def line_step(line, k):
        for p in range(line[1]):
            line_part(line, k, p)

    def line_drain(line):
        copy, parts = line
        for k in range(time_count):
            for p in range(parts):
                @pl.when((z >= k) & (z < last))
                def _():
                    copy(z - k, 0, k, p).wait_send()

                @pl.when((z + k <= last) & (z > 0))
                def _():
                    copy(z + k, 1, k, p).wait_send()

    def x_of(q):
        return functools.partial(x_copy, q), PARTS

    t_line = t_copy, 1

    def pair_copy(q, j, d):
        return rcopy(pair_out.at[d, j], pair_in.at[q, d, j], ps_sem.at[d, j], pr_sem.at[q, d, j], space=partner)

    def chip_copy(q, j, d):
        return rcopy(
            chip_out.at[d - 1, j], chip_in.at[q, d - 1, j], cs_sem.at[d - 1, j], cr_sem.at[q, d - 1, j], space=peer(d)
        )

    def spectrum(q, j, c):
        at = pl.ds(pl.multiple_of(c * own, own), own)
        return jnp.dot(series[q, j], basis[:, at], preferred_element_type=F32)

    def spectral(q, j, send=True):
        @pl.loop(0, pairs)
        def _(n):
            d = pairs - 1 - n
            if q > 0:
                pair_copy(q - 1, j, d).wait_send()
            pair_out[d, j] = spectrum(q, j, 2 * chip_at(d) + 1 - core).astype(BF16)
            pair_copy(q, j, d).start()

        @pl.loop(0, pairs)
        def _(n):
            d = pairs - 1 - n
            value = spectrum(q, j, peer(d))
            pair_copy(q, j, d).wait_recv()
            value = value + pair_in[q, d, j].astype(F32)

            @pl.when(d > 0)
            def _():
                if q > 0:
                    chip_copy(q - 1, j, d).wait_send()
                chip_out[d - 1, j] = value.astype(BF16)
                if send:
                    chip_copy(q, j, d).start()

            @pl.when(d == 0)
            def _():
                mine[q, j] = value

    def spectral_side(q, k, side):
        j = jnp.where(2 * z < time_count, z + k * (1 - 2 * side), z + k * (2 * side - 1))

        @pl.when((j >= 0) & (j <= last))
        def _():
            spectral(q, j)

    def spectral_step(q, k, send=True):
        @pl.loop(0, 2)
        def _(side):
            j = z + k * (2 * side - 1)

            @pl.when((j >= 0) & (j <= last))
            def _():
                spectral(q, j, send)

    def spectral_flush(q, k):
        @pl.loop(0, 2)
        def _(side):
            j = z + k * (2 * side - 1)

            @pl.when((j >= 0) & (j <= last))
            def _():
                for d in reversed(range(1, pairs)):
                    chip_copy(q, j, d).start()

    bits = [1 << b for b in range(pairs.bit_length() - 1)]
    near = [d for d in range(1, pairs) if d in bits]
    turns = [(e, f) for e in bits for f in bits if e != f]
    far = [d for d in range(1, pairs) if d not in bits]
    direct = [d for d in far if d not in [e ^ f for e, f in turns]]

    def piece(q, j, h):
        rows = pl.ds(h * (times // 2), times // 2)
        return scaled.at[q, rows, pl.ds(pl.multiple_of(j * own, own), own)]

    def gather_copy(q, d, h):
        return rcopy(
            piece(q, me, h), piece(q, me, h), gs_sem.at[q, d - 1, h], gr_sem.at[q, me, h], space=peer(d)
        )

    def turn_copy(q, e, f):
        h = 0 if e < f else 1
        at = piece(q, peer(e), h)
        return rcopy(at, at, gs_sem.at[q, (e ^ f) - 1, h], gr_sem.at[q, peer(e), h], space=peer(f))

    def forward_copy(q, j, d, h):
        return rcopy(piece(q, j, h), piece(q, j, h), fs_sem.at[q, d, h], gr_sem.at[q, j, h], space=partner)

    def scale_own(q):
        @pl.loop(0, time_count)
        def _(j):
            for d in range(1, pairs):
                chip_copy(q, j, d).wait_recv()

        value = mine[q]
        for d in range(1, pairs):
            value = value + chip_in[q, d - 1].astype(F32)
        value = value.reshape(time_count * time_local, own)
        rotation = tbasis[...].reshape(time_count * time_local, times)
        turned = lax.dot_general(rotation, value.astype(BF16), CONTRACT_FIRST, preferred_element_type=F32)
        times_eig = jnp.transpose(jnp.broadcast_to(time_eig_ref[...], (8, times)))[:, :1]
        first = pl.multiple_of((z * space_count + me) * own, own)
        turned = turned / (times_eig * space_eig_ref[:, pl.ds(first, own)] + 0.1)
        scaled[q, :, pl.ds(pl.multiple_of(me * own, own), own)] = turned.astype(BF16)
        for h in range(2):
            for d in near + direct:
                gather_copy(q, d, h).start()
            forward_copy(q, me, 0, h).start()

    def gather_near(q):
        for h in range(2):
            for e in near:
                forward_copy(q, peer(e), e, h).wait_recv()
                for f in near:
                    if f != e and h == (0 if e < f else 1):
                        turn_copy(q, e, f).start()
                forward_copy(q, peer(e), e, h).start()

    def gather_far(q):
        for h in range(2):
            for d in far:
                forward_copy(q, peer(d), d, h).wait_recv()
                forward_copy(q, peer(d), d, h).start()

    def gather_finish(q):
        for d in range(pairs):
            for h in range(2):
                forward_copy(q, peer(d) + 1 - 2 * core, d, h).wait_recv()

    def gather_drain(q):
        for h in range(2):
            for d in near + direct:
                gather_copy(q, d, h).wait_send()
            for d in range(pairs):
                forward_copy(q, peer(d), d, h).wait_send()
        for e, f in turns:
            turn_copy(q, e, f).wait_send()

    def back(q, i):
        low = lax.div(i, 2)
        side = lax.rem(i, 2)
        side = jnp.where(2 * z < time_count, side, 1 - side)
        sub = jnp.where(side == 0, last - low, low)
        value = lax.dot_general(
            basis[pl.ds(pl.multiple_of(sub * sub_rows, sub_rows), sub_rows), :],
            scaled[q],
            CONTRACT_LAST,
            preferred_element_type=F32,
        )
        partial[q, pl.ds(sub * PIECES, PIECES)] = value.reshape(PIECES, block_rows, times)

    def up_copy(n, q, m):
        slot = lax.rem(n, RING)
        return rcopy(up_out.at[slot], below.at[q, m], us_sem.at[slot], ur_sem.at[n], tm=z + 1)

    def down_copy(n, q, m):
        slot = lax.rem(n, RING)
        return rcopy(down_out.at[slot], above.at[q, m], ds_sem.at[slot], dr_sem.at[n], tm=z - 1)

    def row_copy(q, m):
        return pltpu.make_async_copy(below.at[q, m], rows_hbm.at[q, m], os_sem.at[q * blocks + m])

    def column_copy(q, p, d):
        source = below.at[q, z * PIECES + p]
        return rcopy(source, cols_hbm.at[q, me, p], ks_sem.at[q, p, d], kr_sem.at[q, me, p], space=peer(d))

    def column_pair(q, p):
        source = below.at[q, z * PIECES + p]
        return rcopy(source, cols_hbm.at[q, me, p], kf_sem.at[q, p, 0], kr_sem.at[q, me, p], space=partner)

    def column_own(q, p):
        return pltpu.make_async_copy(below.at[q, z * PIECES + p], cols_hbm.at[q, me, p], ko_sem.at[q, p])

    def column_forward(q, p, j, d):
        at = cols_hbm.at[q, j, p]
        return rcopy(at, at, kf_sem.at[q, p, d], kr_sem.at[q, j, p], space=partner)

    def columns_start(q, p):
        for d in reversed(range(1, pairs)):
            column_copy(q, p, d).start()
        column_pair(q, p).start()
        column_own(q, p).start()

    def columns_relay(q):
        @pl.loop(0, PIECES)
        def _(n):
            p = jnp.where(2 * z < time_count, PIECES - 1 - n, n)
            p = jnp.where((z == 0) | (z == last), PIECES - 1 - p, p)
            for d in range(1, pairs):
                column_forward(q, p, peer(d), d).wait_recv()
                column_forward(q, p, peer(d), d).start()

    def columns_finish(q):
        @pl.loop(0, PIECES)
        def _(p):
            for d in range(pairs):
                column_forward(q, p, peer(d) + 1 - 2 * core, d).wait_recv()
            for d in range(1, pairs):
                column_copy(q, p, d).wait_send()
                column_forward(q, p, peer(d), d).wait_send()
            column_pair(q, p).wait_send()
            column_own(q, p).wait()

    def finish_block(q, m):
        below[q, m] = (partial[q, m] + below[q, m].astype(F32) + above[q, m].astype(F32)).astype(BF16)
        row_copy(q, m).start()

        @pl.when((lax.div(m, PIECES) == z) & (q == reps - 1))
        def _():
            columns_start(q, lax.rem(m, PIECES))

    def up_step(n):
        at = n - LAG * z

        @pl.when((at >= 0) & (at < total))
        def _():
            q = lax.div(at, blocks)
            m = blocks - 1 - lax.rem(at, blocks)

            @pl.when(z > 0)
            def _():
                up_copy(at, q, m).wait_recv()

            @pl.when(z < last)
            def _():
                @pl.when(at >= RING)
                def _():
                    up_copy(at, q, m).wait_send()

                @pl.when(z == 0)
                def _():
                    up_out[lax.rem(at, RING)] = partial[q, m].astype(BF16)

                @pl.when(z > 0)
                def _():
                    up_out[lax.rem(at, RING)] = (partial[q, m] + below[q, m].astype(F32)).astype(BF16)

                up_copy(at, q, m).start()

            @pl.when((z == last) | ((z > 0) & (q * blocks + m + LAG * (last - z) < n)))
            def _():
                finish_block(q, m)

    def down_step(n):
        at = n - LAG * (last - z)

        @pl.when((at >= 0) & (at < total))
        def _():
            q = lax.div(at, blocks)
            m = lax.rem(at, blocks)

            @pl.when(z < last)
            def _():
                down_copy(at, q, m).wait_recv()

            @pl.when(z > 0)
            def _():
                @pl.when(at >= RING)
                def _():
                    down_copy(at, q, m).wait_send()

                @pl.when(z == last)
                def _():
                    down_out[lax.rem(at, RING)] = partial[q, m].astype(BF16)

                @pl.when(z < last)
                def _():
                    down_out[lax.rem(at, RING)] = (partial[q, m] + above[q, m].astype(F32)).astype(BF16)

                down_copy(at, q, m).start()

            @pl.when((z == 0) | ((z < last) & (q * blocks + blocks - 1 - m + LAG * z <= n)))
            def _():
                finish_block(q, m)

    for load in loads:
        load.wait()
    line_start(x_of(0))
    load_basis.start()
    load_tbasis.wait()
    line_start(t_line)
    load_basis.wait()
    spectral(0, z)
    work = [functools.partial(spectral, q, z) for q in range(1, reps)]
    for k in range(1, time_count):
        for p in range(PARTS):
            if work and k > 1:
                work.pop(0)()
            line_part(x_of(0), k, p)
            if p == PARTS - 1:
                line_step(t_line, k)
                if k == max(1, time_count - 2):
                    for q in range(1, reps):
                        line_start(x_of(q))
            if work and k == 1:
                work.pop(0)()
        while work:
            work.pop(0)()
        work = [functools.partial(spectral_side, 0, k, side) for side in range(2)]
    while work:
        work.pop(0)()
    for d in range(1, pairs):
        t_share(d).start()
    for q in range(reps - 1):
        if q == 0:
            for d in range(1, pairs):
                t_share(d).wait_recv()
        scale_own(q)
        line_step(x_of(q + 1), 1)
        spectral_step(q + 1, 1, False)
        gather_near(q)
        spectral_flush(q + 1, 1)
        for k in range(2, time_count - 1):
            line_step(x_of(q + 1), k)
            spectral_step(q + 1, k)
        gather_far(q)

    ahead = max(7 * blocks // 16, time_count)

    @pl.loop(0, total + LAG * last)
    def _(n):
        q = lax.div(n, blocks)
        i = lax.rem(n, blocks)

        @pl.when((q < reps) & (i < time_count))
        def _():
            @pl.when(i == 0)
            def _():
                gather_finish(q)

            back(q, i)

        up_step(n)
        down_step(n)

        @pl.when((q < reps - 1) & (i == time_count - 1))
        def _():
            for r in range(1, reps):
                @pl.when(q == r - 1)
                def _():
                    for k in range(max(2, time_count - 1), time_count):
                        line_step(x_of(r), k)
                        spectral_step(r, k)

        @pl.when(n == ahead)
        def _():
            scale_own(reps - 1)

        @pl.when(n == (reps - 1) * blocks - 3)
        def _():
            gather_near(reps - 1)

        @pl.when(n == (reps - 1) * blocks - 1)
        def _():
            gather_far(reps - 1)

            @pl.loop(0, PIECES)
            def _(p):
                for r in range(reps - 1):
                    columns_start(r, p)

        @pl.when(n == total - 1)
        def _():
            for r in range(reps - 1):
                columns_relay(r)

    columns_relay(reps - 1)
    for q in range(reps):
        columns_finish(q)
        line_drain(x_of(q))
        gather_drain(q)
    line_drain(t_line)
    for d in range(1, pairs):
        t_share(d).wait_send()
    @pl.loop(0, time_count)
    def _(j):
        for d in range(pairs):
            pair_copy(reps - 1, j, d).wait_send()
            if d > 0:
                chip_copy(reps - 1, j, d).wait_send()

    @pl.loop(0, total)
    def _(n):
        row_copy(lax.div(n, blocks), lax.rem(n, blocks)).wait()

    for n in range(total - min(RING, total), total):
        q, m = n // blocks, n % blocks

        @pl.when(z < last)
        def _():
            up_copy(n, q, m).wait_send()

        @pl.when(z > 0)
        def _():
            down_copy(n, q, m).wait_send()


def solve_field(series, basis, tbasis, time_eig, space_eig, space_count, time_count):
    reps, time_local, rows = series.shape
    depth = basis.shape[1]
    times = tbasis.shape[1]
    own = depth // space_count
    pairs = space_count // 2
    blocks = PIECES * time_count
    block_rows = rows // blocks
    dma = pltpu.SemaphoreType.DMA
    hbm = pl.BlockSpec(memory_space=pl.ANY)
    vmem = pl.BlockSpec(memory_space=pltpu.VMEM)
    return pl.pallas_call(
        functools.partial(field_kernel, space_count, time_count),
        out_shape=(
            jax.ShapeDtypeStruct((reps, blocks, block_rows, times), BF16),
            jax.ShapeDtypeStruct((reps, space_count, PIECES, block_rows, times), BF16),
        ),
        in_specs=[hbm, hbm, hbm, vmem, vmem],
        out_specs=(hbm, hbm),
        scratch_shapes=[
            pltpu.VMEM((rows, depth), BF16),
            pltpu.VMEM((reps, time_count, time_local, rows), BF16),
            pltpu.VMEM((time_count, time_local, times), BF16),
            pltpu.VMEM((pairs, time_count, time_local, own), BF16),
            pltpu.VMEM((reps, pairs, time_count, time_local, own), BF16),
            pltpu.VMEM((pairs - 1, time_count, time_local, own), BF16),
            pltpu.VMEM((reps, pairs - 1, time_count, time_local, own), BF16),
            pltpu.VMEM((reps, time_count, time_local, own), F32),
            pltpu.VMEM((reps, times, depth), BF16),
            pltpu.VMEM((reps, blocks, block_rows, times), F32),
            pltpu.VMEM((reps, blocks, block_rows, times), BF16),
            pltpu.VMEM((reps, blocks, block_rows, times), BF16),
            pltpu.VMEM((RING, block_rows, times), BF16),
            pltpu.VMEM((RING, block_rows, times), BF16),
            dma((2 + reps,)),
            dma((reps, 2, time_count, PARTS)),
            dma((reps, time_count, PARTS)),
            dma((2, time_count)),
            dma((time_count,)),
            dma((2, pairs)),
            dma((pairs, time_count)),
            dma((reps, pairs, time_count)),
            dma((pairs - 1, time_count)),
            dma((reps, pairs - 1, time_count)),
            dma((reps, pairs - 1, 2)),
            dma((reps, space_count, 2)),
            dma((reps, pairs, 2)),
            dma((RING,)),
            dma((reps * blocks,)),
            dma((RING,)),
            dma((reps * blocks,)),
            dma((reps * blocks,)),
            dma((reps, PIECES, pairs)),
            dma((reps, space_count, PIECES)),
            dma((reps, PIECES, pairs)),
            dma((reps, PIECES)),
        ],
        compiler_params=pltpu.CompilerParams(
            collective_id=0, has_side_effects=True, vmem_limit_bytes=VMEM_BYTES
        ),
    )(series, basis, tbasis, time_eig, space_eig)


def grad_kernel(reps, scale, *refs):
    rows, columns = refs[:reps], refs[reps : 2 * reps]
    eig_ref, basis_ref, alpha_ref, grad_ref, alpha_scr, grad_scr, weighted_scr = refs[2 * reps :]
    tile, blocks, _ = grad_ref.shape
    for q in range(reps):
        block = rows[q][0]
        weighted_scr[q] = (block.astype(F32) * eig_ref[...] / scale).astype(BF16)
        alpha_scr[pl.ds(q, tile, stride=reps), :] = lax.dot_general(
            block, basis_ref[...], CONTRACT_LAST, preferred_element_type=F32
        )
    alpha_ref[...] = alpha_scr[...].astype(BF16).reshape(alpha_ref.shape)

    sub = columns[0].shape[2]
    @pl.loop(0, blocks)
    def _(a):
        total = None
        for q in range(reps):
            part = lax.dot_general(
                weighted_scr[q], columns[q][0, a], CONTRACT_LAST, preferred_element_type=F32
            )
            total = part if total is None else total + part
        for w in range(0, sub, 128):
            grad_scr[w // 128, pl.ds(a, tile, stride=blocks), :] = total[:, w : w + 128]
    for w in range(0, sub, 128):
        grad_ref[:, :, w : w + 128] = (
            grad_scr[w // 128].astype(BF16).reshape(tile, blocks, 128)
        )


def grad_and_alpha(rows, columns, time_eig, time_basis):
    reps, row_count, times = rows.shape
    _, blocks, sub, _ = columns.shape
    time_local = time_basis.shape[0]
    tile = min(row_count, 512)
    row_specs = [pl.BlockSpec((1, tile, times), lambda i, q=q: (q, i, 0)) for q in range(reps)]
    col_specs = [pl.BlockSpec((1, blocks, sub, times), lambda i, q=q: (q, 0, 0, 0)) for q in range(reps)]
    return pl.pallas_call(
        lambda *refs: grad_kernel(reps, reps * times, *refs),
        out_shape=(
            jax.ShapeDtypeStruct((row_count, reps, time_local), BF16),
            jax.ShapeDtypeStruct((row_count, blocks, sub), BF16),
        ),
        grid=(row_count // tile,),
        in_specs=row_specs
        + col_specs
        + [
            pl.BlockSpec((1, times), lambda i: (0, 0)),
            pl.BlockSpec((time_local, times), lambda i: (0, 0)),
        ],
        out_specs=(
            pl.BlockSpec((tile, reps, time_local), lambda i: (i, 0, 0)),
            pl.BlockSpec((tile, blocks, sub), lambda i: (i, 0, 0)),
        ),
        scratch_shapes=[
            pltpu.VMEM((tile * reps, time_local), F32),
            pltpu.VMEM((sub // 128, tile * blocks, 128), F32),
            pltpu.VMEM((reps, tile, times), BF16),
        ],
    )(*[rows] * reps, *[columns] * reps, time_eig[None, :], time_basis)


def per_device(series, space_basis, time_basis, space_eig, time_eig):
    space_count = lax.axis_size("space")
    time_count = lax.axis_size("tm")
    rows, columns = solve_field(
        jnp.transpose(series, (1, 2, 0)),
        space_basis,
        time_basis,
        time_eig[None, :],
        space_eig[None, :],
        space_count,
        time_count,
    )
    reps, times = rows.shape[0], rows.shape[-1]
    return grad_and_alpha(
        rows.reshape(reps, -1, times), columns.reshape(reps, space_count, -1, times), time_eig, time_basis
    )


def solution(mesh):
    return jax.shard_map(
        per_device,
        mesh=mesh,
        in_specs=(P("space", None, "tm"), P("space", "tm"), P("tm", None), P(), P()),
        out_specs=(P("space", None, "tm"), P("space", None, "tm")),
        check_vma=False,
    )
```

time: 303 us -> 245 us (0.81)
  Pallas kernels: 295 us -> 240 us
    pallas_call x1, Pallas kernels: 256 us -> 200 us  [solve_field(): pl.pallas_call(functools.partial(field_kernel, space_count, time_count),...]
where the time goes in v1:
time: 245 us; the launch traced here: 244 us
  Pallas kernels  240 us (98%)
  local copies, waits for them, and re-layouts  3.66 us (1%)
    pallas_call x1, Pallas kernels, solve_field(): pl.pallas_call(functools.partial(field_kernel, space_count, time_count),...  200 us
    pallas_call x1, Pallas kernels, grad_and_alpha(): pl.pallas_call(lambda *refs: grad_kernel(reps, reps * times, *refs), out_...  39.8 us

profile of v1, /device:TPU:0, one launch (start us, length us, event | category | flops | bytes accessed | tf_op | source)
XLA Modules:
  0.0 244.5 jit_solution(15624394003608545527)
XLA Ops:
  0.6 3.7 %copy.7 = bf16[2048,2,128]{0,2,1:T(8,128)(2,1)} copy(bf16[2048,2,128]{2,1,0:T(2,128)(2,1)} %param.5) | data formatting | bytes 2097152 | tf_op args[0]
  4.3 200.4 %shard_map.68 = (bf16[2,16,128,512]{3,2,1,0:T(8,128)(2,1)}, bf16[2,8,4,128,512]{4,3,2,1,0:T(8,128)(2,1)}) custom-call(bf16[2,128,2048]{2,1,0:T(8,128)(2,1)} %bitcast.9, bf16[2048,4096]{1,0:T(8,128)(2,1)} %basis_hbm.1, bf16[128,512]{1,0:T(8,128)(2,1)} %refs_5_.1, f32[1,512]{1,0:T(1,128)} %bitcast.11, f32[1,16384]{1,0:T(1,128)} %bitcast.10), custom_call_target="tpu_custom_call" | custom-call | tf_op jit(solution)/shard_map/pallas_call | solution.py:570
  204.7 39.8 %shard_map.69 = (bf16[2048,2,128]{2,1,0:T(2,128)(2,1)}, bf16[2048,8,512]{2,1,0:T(8,128)(2,1)}) custom-call(bf16[2,2048,512]{2,1,0:T(8,128)(2,1)} %bitcast.7, bf16[2,2048,512]{2,1,0:T(8,128)(2,1)} %bitcast.8, bf16[2,8,512,512]{3,2,1,0:T(8,128)(2,1)} %bitcast.5, bf16[2,8,512,512]{3,2,1,0:T(8,128)(2,1)} %bitcast.6, f32[1,512]{1,0:T(1,128)} %bitcast.12, ...), custom_call_target="tpu_custom_call" | custom-call | tf_op jit(solution)/shard_map/pallas_call | solution.py:658

commit v2 on v1

--- a/solution.py
+++ b/solution.py
@@ -103,9 +103,25 @@
         at = tbasis.at[j, own_share]
         return rcopy(at, at, ts_sem.at[way, step], tr_sem.at[j], tm=z + 1 - 2 * way)
 
-    def t_share(d):
-        at = tbasis.at[:, own_share]
-        return rcopy(at, at, te_sem.at[0, d], te_sem.at[1, d], space=peer(d))
+    def t_share(j, d):
+        at = tbasis.at[j, own_share]
+        return rcopy(at, at, te_sem.at[0, d, j], te_sem.at[1, d, j], space=peer(d))
+
+    def t_share_step(k):
+        @pl.loop(0, 1 if k == 0 else 2)
+        def _(side):
+            j = z + k * (2 * side - 1)
+
+            @pl.when((j >= 0) & (j <= last))
+            def _():
+                for d in range(1, pairs):
+                    t_share(j, d).start()
+
+    def t_share_each(act):
+        @pl.loop(0, time_count)
+        def _(j):
+            for d in range(1, pairs):
+                act(t_share(j, d))
 
     def line_start(line):
         copy, parts = line
@@ -318,22 +334,28 @@
         slot = lax.rem(n, RING)
         return rcopy(down_out.at[slot], above.at[q, m], ds_sem.at[slot], dr_sem.at[n], tm=z - 1)
 
+    def rep_columns(q):
+        return pl.ds(pl.multiple_of(q * times, times), times)
+
     def row_copy(q, m):
-        return pltpu.make_async_copy(below.at[q, m], rows_hbm.at[q, m], os_sem.at[q * blocks + m])
+        return pltpu.make_async_copy(below.at[q, m], rows_hbm.at[m, :, rep_columns(q)], os_sem.at[q * blocks + m])
+
+    def column_at(q, p, j):
+        return cols_hbm.at[j, p, :, rep_columns(q)]
 
     def column_copy(q, p, d):
         source = below.at[q, z * PIECES + p]
-        return rcopy(source, cols_hbm.at[q, me, p], ks_sem.at[q, p, d], kr_sem.at[q, me, p], space=peer(d))
+        return rcopy(source, column_at(q, p, me), ks_sem.at[q, p, d], kr_sem.at[q, me, p], space=peer(d))
 
     def column_pair(q, p):
         source = below.at[q, z * PIECES + p]
-        return rcopy(source, cols_hbm.at[q, me, p], kf_sem.at[q, p, 0], kr_sem.at[q, me, p], space=partner)
+        return rcopy(source, column_at(q, p, me), kf_sem.at[q, p, 0], kr_sem.at[q, me, p], space=partner)
 
     def column_own(q, p):
-        return pltpu.make_async_copy(below.at[q, z * PIECES + p], cols_hbm.at[q, me, p], ko_sem.at[q, p])
+        return pltpu.make_async_copy(below.at[q, z * PIECES + p], column_at(q, p, me), ko_sem.at[q, p])
 
     def column_forward(q, p, j, d):
-        at = cols_hbm.at[q, j, p]
+        at = column_at(q, p, j)
         return rcopy(at, at, kf_sem.at[q, p, d], kr_sem.at[q, j, p], space=partner)
 
     def columns_start(q, p):
@@ -440,6 +462,7 @@
     load_basis.start()
     load_tbasis.wait()
     line_start(t_line)
+    t_share_step(0)
     load_basis.wait()
     spectral(0, z)
     work = [functools.partial(spectral, q, z) for q in range(1, reps)]
@@ -450,6 +473,7 @@
             line_part(x_of(0), k, p)
             if p == PARTS - 1:
                 line_step(t_line, k)
+                t_share_step(k)
                 if k == max(1, time_count - 2):
                     for q in range(1, reps):
                         line_start(x_of(q))
@@ -460,12 +484,9 @@
         work = [functools.partial(spectral_side, 0, k, side) for side in range(2)]
     while work:
         work.pop(0)()
-    for d in range(1, pairs):
-        t_share(d).start()
     for q in range(reps - 1):
         if q == 0:
-            for d in range(1, pairs):
-                t_share(d).wait_recv()
+            t_share_each(lambda copy: copy.wait_recv())
         scale_own(q)
         line_step(x_of(q + 1), 1)
         spectral_step(q + 1, 1, False)
@@ -531,8 +552,7 @@
         line_drain(x_of(q))
         gather_drain(q)
     line_drain(t_line)
-    for d in range(1, pairs):
-        t_share(d).wait_send()
+    t_share_each(lambda copy: copy.wait_send())
     @pl.loop(0, time_count)
     def _(j):
         for d in range(pairs):
@@ -570,8 +590,8 @@
     return pl.pallas_call(
         functools.partial(field_kernel, space_count, time_count),
         out_shape=(
-            jax.ShapeDtypeStruct((reps, blocks, block_rows, times), BF16),
-            jax.ShapeDtypeStruct((reps, space_count, PIECES, block_rows, times), BF16),
+            jax.ShapeDtypeStruct((blocks, block_rows, reps * times), BF16),
+            jax.ShapeDtypeStruct((space_count, PIECES, block_rows, reps * times), BF16),
         ),
         in_specs=[hbm, hbm, hbm, vmem, vmem],
         out_specs=(hbm, hbm),
@@ -595,7 +615,7 @@
             dma((reps, time_count, PARTS)),
             dma((2, time_count)),
             dma((time_count,)),
-            dma((2, pairs)),
+            dma((2, pairs, time_count)),
             dma((pairs, time_count)),
             dma((reps, pairs, time_count)),
             dma((pairs - 1, time_count)),
@@ -619,53 +639,45 @@
     )(series, basis, tbasis, time_eig, space_eig)
 
 
-def grad_kernel(reps, scale, *refs):
-    rows, columns = refs[:reps], refs[reps : 2 * reps]
-    eig_ref, basis_ref, alpha_ref, grad_ref, alpha_scr, grad_scr, weighted_scr = refs[2 * reps :]
-    tile, blocks, _ = grad_ref.shape
+def grad_kernel(reps, wide, rows, columns, eig_ref, basis_ref, alpha_ref, grad_ref, alpha_scr, weighted, *halves):
+    tile, blocks, sub = grad_ref.shape
+    depth = rows.shape[1]
+    times = depth // reps
+    weighted[...] = (rows[...].astype(F32) * eig_ref[...] / depth).astype(BF16)
     for q in range(reps):
-        block = rows[q][0]
-        weighted_scr[q] = (block.astype(F32) * eig_ref[...] / scale).astype(BF16)
         alpha_scr[pl.ds(q, tile, stride=reps), :] = lax.dot_general(
-            block, basis_ref[...], CONTRACT_LAST, preferred_element_type=F32
+            rows[:, q * times : (q + 1) * times], basis_ref[...], CONTRACT_LAST, preferred_element_type=F32
         )
     alpha_ref[...] = alpha_scr[...].astype(BF16).reshape(alpha_ref.shape)
-
-    sub = columns[0].shape[2]
-    @pl.loop(0, blocks)
-    def _(a):
-        total = None
-        for q in range(reps):
+    for w in range(0, sub, wide):
+        half = halves[w // wide % 2]
+        for a in range(blocks):
             part = lax.dot_general(
-                weighted_scr[q], columns[q][0, a], CONTRACT_LAST, preferred_element_type=F32
+                weighted[...], columns[a, w : w + wide, :], CONTRACT_LAST, preferred_element_type=F32
             )
-            total = part if total is None else total + part
-        for w in range(0, sub, 128):
-            grad_scr[w // 128, pl.ds(a, tile, stride=blocks), :] = total[:, w : w + 128]
-    for w in range(0, sub, 128):
-        grad_ref[:, :, w : w + 128] = (
-            grad_scr[w // 128].astype(BF16).reshape(tile, blocks, 128)
-        )
-
-
-def grad_and_alpha(rows, columns, time_eig, time_basis):
-    reps, row_count, times = rows.shape
-    _, blocks, sub, _ = columns.shape
-    time_local = time_basis.shape[0]
-    tile = min(row_count, 512)
-    row_specs = [pl.BlockSpec((1, tile, times), lambda i, q=q: (q, i, 0)) for q in range(reps)]
-    col_specs = [pl.BlockSpec((1, blocks, sub, times), lambda i, q=q: (q, 0, 0, 0)) for q in range(reps)]
+            for v in range(0, wide, 128):
+                half[v // 128, pl.ds(a, tile, stride=blocks), :] = part[:, v : v + 128]
+        for v in range(0, wide, 128):
+            grad_ref[:, :, w + v : w + v + 128] = half[v // 128].astype(BF16).reshape(tile, blocks, 128)
+
+
+def grad_and_alpha(rows, columns, time_eig, time_basis, reps):
+    row_count, depth = rows.shape
+    blocks, sub, _ = columns.shape
+    time_local, times = time_basis.shape
+    tile = min(row_count, 256)
+    wide = min(sub, 256)
     return pl.pallas_call(
-        lambda *refs: grad_kernel(reps, reps * times, *refs),
+        functools.partial(grad_kernel, reps, wide),
         out_shape=(
             jax.ShapeDtypeStruct((row_count, reps, time_local), BF16),
             jax.ShapeDtypeStruct((row_count, blocks, sub), BF16),
         ),
         grid=(row_count // tile,),
-        in_specs=row_specs
-        + col_specs
-        + [
-            pl.BlockSpec((1, times), lambda i: (0, 0)),
+        in_specs=[
+            pl.BlockSpec((tile, depth), lambda i: (i, 0)),
+            pl.BlockSpec((blocks, sub, depth), lambda i: (0, 0, 0)),
+            pl.BlockSpec((1, depth), lambda i: (0, 0)),
             pl.BlockSpec((time_local, times), lambda i: (0, 0)),
         ],
         out_specs=(
@@ -674,10 +686,11 @@
         ),
         scratch_shapes=[
             pltpu.VMEM((tile * reps, time_local), F32),
-            pltpu.VMEM((sub // 128, tile * blocks, 128), F32),
-            pltpu.VMEM((reps, tile, times), BF16),
+            pltpu.VMEM((tile, depth), BF16),
+            pltpu.VMEM((wide // 128, tile * blocks, 128), F32),
+            pltpu.VMEM((wide // 128, tile * blocks, 128), F32),
         ],
-    )(*[rows] * reps, *[columns] * reps, time_eig[None, :], time_basis)
+    )(rows, columns, jnp.tile(time_eig, reps)[None, :], time_basis)
 
 
 def per_device(series, space_basis, time_basis, space_eig, time_eig):
@@ -692,9 +705,9 @@
         space_count,
         time_count,
     )
-    reps, times = rows.shape[0], rows.shape[-1]
+    depth = rows.shape[-1]
     return grad_and_alpha(
-        rows.reshape(reps, -1, times), columns.reshape(reps, space_count, -1, times), time_eig, time_basis
+        rows.reshape(-1, depth), columns.reshape(space_count, -1, depth), time_eig, time_basis, series.shape[1]
     )
 
 

time: 245 us -> 230 us (0.939)
  Pallas kernels: 240 us -> 224 us
    pallas_call x1, Pallas kernels: 39.8 us -> 29.3 us  [grad_and_alpha(): pl.pallas_call(functools.partial(grad_kernel, reps, wide), out_shape=(jax...]
    pallas_call x1, Pallas kernels: 200 us -> 195 us  [solve_field(): pl.pallas_call(functools.partial(field_kernel, space_count, time_count),...]
    unnamed x1 -> x3, local copies, waits for them, and re-layouts: 3.66 us -> 4.94 us
where the time goes in v2:
time: 230 us
  Pallas kernels  224 us (97%)
  local copies, waits for them, and re-layouts  4.94 us (2%)
    pallas_call x1, Pallas kernels, solve_field(): pl.pallas_call(functools.partial(field_kernel, space_count, time_count),...  195 us
    pallas_call x1, Pallas kernels, grad_and_alpha(): pl.pallas_call(functools.partial(grad_kernel, reps, wide), out_shape=(jax...  29.3 us
    unnamed x3, local copies, waits for them, and re-layouts  4.94 us

profile of v2, /device:TPU:0, one launch (start us, length us, event | category | flops | bytes accessed | tf_op | source)
XLA Modules:
  0.0 230.0 jit_solution(11761665599511199850)
XLA Ops:
  0.6 0.7 broadcast_bitcast_fusion
  1.3 0.6 copy.8
  1.9 3.7 %copy.7 = bf16[2048,2,128]{0,2,1:T(8,128)(2,1)} copy(bf16[2048,2,128]{2,1,0:T(2,128)(2,1)} %param.5) | data formatting | bytes 2097152 | tf_op args[0]
  5.6 195.2 %shard_map.68 = (bf16[16,128,1024]{2,1,0:T(8,128)(2,1)}, bf16[8,4,128,1024]{3,2,1,0:T(8,128)(2,1)}) custom-call(bf16[2,128,2048]{2,1,0:T(8,128)(2,1)} %bitcast.10, bf16[2048,4096]{1,0:T(8,128)(2,1)} %basis_hbm.1, bf16[128,512]{1,0:T(8,128)(2,1)} %basis_ref.1, f32[1,512]{1,0:T(1,128)} %bitcast.14, f32[1,16384]{1,0:T(1,128)} %bitcast.12), custom_call_target="tpu_custom_call" | custom-call | tf_op jit(solution)/shard_map/pallas_call | solution.py:590
  200.7 29.3 %shard_map.69 = (bf16[2048,2,128]{2,1,0:T(2,128)(2,1)}, bf16[2048,8,512]{2,1,0:T(8,128)(2,1)}) custom-call(bf16[2048,1024]{1,0:T(8,128)(2,1)} %bitcast.11, bf16[8,512,1024]{2,1,0:T(8,128)(2,1)} %bitcast.9, f32[1,1024]{1,0:T(1,128)} %bitcast.13, bf16[128,512]{1,0:T(8,128)(2,1)} %basis_ref.1), custom_call_target="tpu_custom_call" | custom-call | tf_op jit(solution)/shard_map/pallas_call | solution.py:670

commit v3 on v2

--- a/solution.py
+++ b/solution.py
@@ -14,8 +14,9 @@
 CONTRACT_FIRST = (((0,), (0,)), ((), ()))
 VMEM_BYTES = 67043328
 RING = 4
-PIECES = 4
+PIECES = 2
 PARTS = 2
+HALVES = 2
 LAG = 2
 
 
@@ -40,7 +41,8 @@
     us_sem, ur_sem, ds_sem, dr_sem, os_sem, ks_sem, kr_sem, kf_sem, ko_sem,
 ):
     reps, _, time_local, _ = series.shape
-    _, blocks, block_rows, times = partial.shape
+    streams, blocks, block_rows, width = partial.shape
+    times = width * HALVES
     own = mine.shape[3]
     pairs = space_count // 2
     last = time_count - 1
@@ -50,7 +52,7 @@
     core = lax.rem(me, 2)
     chip = lax.div(me, 2)
     partner = me + 1 - 2 * core
-    total = reps * blocks
+    total = streams * blocks
 
     def chip_at(d):
         return lax.bitwise_xor(chip, d)
@@ -246,22 +248,22 @@
     far = [d for d in range(1, pairs) if d not in bits]
     direct = [d for d in far if d not in [e ^ f for e, f in turns]]
 
-    def piece(q, j, h):
-        rows = pl.ds(h * (times // 2), times // 2)
-        return scaled.at[q, rows, pl.ds(pl.multiple_of(j * own, own), own)]
-
-    def gather_copy(q, d, h):
+    def piece(v, j, g):
+        rows = pl.ds(g * (width // 2), width // 2)
+        return scaled.at[v, rows, pl.ds(pl.multiple_of(j * own, own), own)]
+
+    def gather_copy(v, d, g):
         return rcopy(
-            piece(q, me, h), piece(q, me, h), gs_sem.at[q, d - 1, h], gr_sem.at[q, me, h], space=peer(d)
+            piece(v, me, g), piece(v, me, g), gs_sem.at[v, d - 1, g], gr_sem.at[v, me, g], space=peer(d)
         )
 
-    def turn_copy(q, e, f):
-        h = 0 if e < f else 1
-        at = piece(q, peer(e), h)
-        return rcopy(at, at, gs_sem.at[q, (e ^ f) - 1, h], gr_sem.at[q, peer(e), h], space=peer(f))
-
-    def forward_copy(q, j, d, h):
-        return rcopy(piece(q, j, h), piece(q, j, h), fs_sem.at[q, d, h], gr_sem.at[q, j, h], space=partner)
+    def turn_copy(v, e, f):
+        g = 0 if e < f else 1
+        at = piece(v, peer(e), g)
+        return rcopy(at, at, gs_sem.at[v, (e ^ f) - 1, g], gr_sem.at[v, peer(e), g], space=peer(f))
+
+    def forward_copy(v, j, d, g):
+        return rcopy(piece(v, j, g), piece(v, j, g), fs_sem.at[v, d, g], gr_sem.at[v, j, g], space=partner)
 
     def scale_own(q):
         @pl.loop(0, time_count)
@@ -278,40 +280,45 @@
         times_eig = jnp.transpose(jnp.broadcast_to(time_eig_ref[...], (8, times)))[:, :1]
         first = pl.multiple_of((z * space_count + me) * own, own)
         turned = turned / (times_eig * space_eig_ref[:, pl.ds(first, own)] + 0.1)
-        scaled[q, :, pl.ds(pl.multiple_of(me * own, own), own)] = turned.astype(BF16)
-        for h in range(2):
+        for h in range(HALVES):
+            scaled[q * HALVES + h, :, pl.ds(pl.multiple_of(me * own, own), own)] = turned[
+                h * width : (h + 1) * width
+            ].astype(BF16)
+
+    def gather_start(v):
+        for g in range(2):
             for d in near + direct:
-                gather_copy(q, d, h).start()
-            forward_copy(q, me, 0, h).start()
-
-    def gather_near(q):
-        for h in range(2):
+                gather_copy(v, d, g).start()
+            forward_copy(v, me, 0, g).start()
+
+    def gather_near(v):
+        for g in range(2):
             for e in near:
-                forward_copy(q, peer(e), e, h).wait_recv()
+                forward_copy(v, peer(e), e, g).wait_recv()
                 for f in near:
-                    if f != e and h == (0 if e < f else 1):
-                        turn_copy(q, e, f).start()
-                forward_copy(q, peer(e), e, h).start()
-
-    def gather_far(q):
-        for h in range(2):
+                    if f != e and g == (0 if e < f else 1):
+                        turn_copy(v, e, f).start()
+                forward_copy(v, peer(e), e, g).start()
+
+    def gather_far(v):
+        for g in range(2):
             for d in far:
-                forward_copy(q, peer(d), d, h).wait_recv()
-                forward_copy(q, peer(d), d, h).start()
-
-    def gather_finish(q):
+                forward_copy(v, peer(d), d, g).wait_recv()
+                forward_copy(v, peer(d), d, g).start()
+
+    def gather_finish(v):
         for d in range(pairs):
-            for h in range(2):
-                forward_copy(q, peer(d) + 1 - 2 * core, d, h).wait_recv()
-
-    def gather_drain(q):
-        for h in range(2):
+            for g in range(2):
+                forward_copy(v, peer(d) + 1 - 2 * core, d, g).wait_recv()
+
+    def gather_drain(v):
+        for g in range(2):
             for d in near + direct:
-                gather_copy(q, d, h).wait_send()
+                gather_copy(v, d, g).wait_send()
             for d in range(pairs):
-                forward_copy(q, peer(d), d, h).wait_send()
+                forward_copy(v, peer(d), d, g).wait_send()
         for e, f in turns:
-            turn_copy(q, e, f).wait_send()
+            turn_copy(v, e, f).wait_send()
 
     def back(q, i):
         low = lax.div(i, 2)
@@ -324,7 +331,7 @@
             CONTRACT_LAST,
             preferred_element_type=F32,
         )
-        partial[q, pl.ds(sub * PIECES, PIECES)] = value.reshape(PIECES, block_rows, times)
+        partial[q, pl.ds(sub * PIECES, PIECES)] = value.reshape(PIECES, block_rows, width)
 
     def up_copy(n, q, m):
         slot = lax.rem(n, RING)
@@ -335,7 +342,7 @@
         return rcopy(down_out.at[slot], above.at[q, m], ds_sem.at[slot], dr_sem.at[n], tm=z - 1)
 
     def rep_columns(q):
-        return pl.ds(pl.multiple_of(q * times, times), times)
+        return pl.ds(pl.multiple_of(q * width, width), width)
 
     def row_copy(q, m):
         return pltpu.make_async_copy(below.at[q, m], rows_hbm.at[m, :, rep_columns(q)], os_sem.at[q * blocks + m])
@@ -388,7 +395,7 @@
         below[q, m] = (partial[q, m] + below[q, m].astype(F32) + above[q, m].astype(F32)).astype(BF16)
         row_copy(q, m).start()
 
-        @pl.when((lax.div(m, PIECES) == z) & (q == reps - 1))
+        @pl.when((lax.div(m, PIECES) == z) & (q == streams - 1))
         def _():
             columns_start(q, lax.rem(m, PIECES))
 
@@ -487,70 +494,83 @@
     for q in range(reps - 1):
         if q == 0:
             t_share_each(lambda copy: copy.wait_recv())
+        v = q * HALVES
         scale_own(q)
+        gather_start(v)
         line_step(x_of(q + 1), 1)
         spectral_step(q + 1, 1, False)
-        gather_near(q)
-        spectral_flush(q + 1, 1)
+        gather_near(v)
+        for h in range(1, HALVES):
+            gather_start(v + h)
         for k in range(2, time_count - 1):
             line_step(x_of(q + 1), k)
-            spectral_step(q + 1, k)
-        gather_far(q)
-
-    ahead = max(7 * blocks // 16, time_count)
+            spectral_step(q + 1, k, False)
+        gather_far(v)
+
+    after = {}
+
+    def then(n, act, *args):
+        after.setdefault(n, []).append(functools.partial(act, *args))
+
+    def columns_bulk(v):
+        @pl.loop(0, PIECES)
+        def _(p):
+            columns_start(v, p)
+
+    unit = max(PIECES // 2, 1)
+    for q in range(reps):
+        first = q * HALVES * blocks
+        if q + 1 < reps:
+            then(first + blocks - 5 * unit, gather_near, q * HALVES + 1)
+            for k in range(1, time_count - 1):
+                then(first + blocks - 5 * unit, spectral_flush, q + 1, k)
+            for k in range(max(2, time_count - 1), time_count):
+                then(first + blocks - 2 * unit, line_step, x_of(q + 1), k)
+                then(first + blocks - 2 * unit, spectral_step, q + 1, k)
+        if q > 0:
+            then(first - blocks + 3 * unit, scale_own, q)
+            then(first - blocks + 3 * unit, gather_start, q * HALVES)
+            then(first - 3 * unit, gather_near, q * HALVES)
+            then(first - 1, gather_far, q * HALVES)
+        for h in range(1, HALVES):
+            v = q * HALVES + h
+            if q > 0:
+                then(first - 3 * unit, gather_start, v)
+            if q > 0:
+                then(v * blocks - 6 * unit, gather_near, v)
+            then(v * blocks - 3 * unit, gather_far, v)
+    for v in range(streams - 1):
+        then(max((streams - 1) * blocks - 3 * unit, (v + 1) * blocks), columns_bulk, v)
+    for v in range(streams - 1):
+        then(total - 1 if v < streams - 2 else total + LAG * last - 2 * unit, columns_relay, v)
 
     @pl.loop(0, total + LAG * last)
     def _(n):
-        q = lax.div(n, blocks)
+        v = lax.div(n, blocks)
         i = lax.rem(n, blocks)
 
-        @pl.when((q < reps) & (i < time_count))
+        @pl.when((v < streams) & (i < time_count))
         def _():
             @pl.when(i == 0)
             def _():
-                gather_finish(q)
-
-            back(q, i)
+                gather_finish(v)
+
+            back(v, i)
 
         up_step(n)
         down_step(n)
-
-        @pl.when((q < reps - 1) & (i == time_count - 1))
-        def _():
-            for r in range(1, reps):
-                @pl.when(q == r - 1)
-                def _():
-                    for k in range(max(2, time_count - 1), time_count):
-                        line_step(x_of(r), k)
-                        spectral_step(r, k)
-
-        @pl.when(n == ahead)
-        def _():
-            scale_own(reps - 1)
-
-        @pl.when(n == (reps - 1) * blocks - 3)
-        def _():
-            gather_near(reps - 1)
-
-        @pl.when(n == (reps - 1) * blocks - 1)
-        def _():
-            gather_far(reps - 1)
-
-            @pl.loop(0, PIECES)
-            def _(p):
-                for r in range(reps - 1):
-                    columns_start(r, p)
-
-        @pl.when(n == total - 1)
-        def _():
-            for r in range(reps - 1):
-                columns_relay(r)
-
-    columns_relay(reps - 1)
+        for at, acts in after.items():
+            @pl.when(n == at)
+            def _():
+                for act in acts:
+                    act()
+
+    columns_relay(streams - 1)
+    for v in range(streams):
+        columns_finish(v)
+        gather_drain(v)
     for q in range(reps):
-        columns_finish(q)
         line_drain(x_of(q))
-        gather_drain(q)
     line_drain(t_line)
     t_share_each(lambda copy: copy.wait_send())
     @pl.loop(0, time_count)
@@ -584,6 +604,8 @@
     pairs = space_count // 2
     blocks = PIECES * time_count
     block_rows = rows // blocks
+    streams = reps * HALVES
+    width = times // HALVES
     dma = pltpu.SemaphoreType.DMA
     hbm = pl.BlockSpec(memory_space=pl.ANY)
     vmem = pl.BlockSpec(memory_space=pltpu.VMEM)
@@ -604,12 +626,12 @@
             pltpu.VMEM((pairs - 1, time_count, time_local, own), BF16),
             pltpu.VMEM((reps, pairs - 1, time_count, time_local, own), BF16),
             pltpu.VMEM((reps, time_count, time_local, own), F32),
-            pltpu.VMEM((reps, times, depth), BF16),
-            pltpu.VMEM((reps, blocks, block_rows, times), F32),
-            pltpu.VMEM((reps, blocks, block_rows, times), BF16),
-            pltpu.VMEM((reps, blocks, block_rows, times), BF16),
-            pltpu.VMEM((RING, block_rows, times), BF16),
-            pltpu.VMEM((RING, block_rows, times), BF16),
+            pltpu.VMEM((streams, width, depth), BF16),
+            pltpu.VMEM((streams, blocks, block_rows, width), F32),
+            pltpu.VMEM((streams, blocks, block_rows, width), BF16),
+            pltpu.VMEM((streams, blocks, block_rows, width), BF16),
+            pltpu.VMEM((RING, block_rows, width), BF16),
+            pltpu.VMEM((RING, block_rows, width), BF16),
             dma((2 + reps,)),
             dma((reps, 2, time_count, PARTS)),
             dma((reps, time_count, PARTS)),
@@ -620,18 +642,18 @@
             dma((reps, pairs, time_count)),
             dma((pairs - 1, time_count)),
             dma((reps, pairs - 1, time_count)),
-            dma((reps, pairs - 1, 2)),
-            dma((reps, space_count, 2)),
-            dma((reps, pairs, 2)),
+            dma((streams, pairs - 1, 2)),
+            dma((streams, space_count, 2)),
+            dma((streams, pairs, 2)),
             dma((RING,)),
-            dma((reps * blocks,)),
+            dma((streams * blocks,)),
             dma((RING,)),
-            dma((reps * blocks,)),
-            dma((reps * blocks,)),
-            dma((reps, PIECES, pairs)),
-            dma((reps, space_count, PIECES)),
-            dma((reps, PIECES, pairs)),
-            dma((reps, PIECES)),
+            dma((streams * blocks,)),
+            dma((streams * blocks,)),
+            dma((streams, PIECES, pairs)),
+            dma((streams, space_count, PIECES)),
+            dma((streams, PIECES, pairs)),
+            dma((streams, PIECES)),
         ],
         compiler_params=pltpu.CompilerParams(
             collective_id=0, has_side_effects=True, vmem_limit_bytes=VMEM_BYTES
@@ -643,10 +665,11 @@
     tile, blocks, sub = grad_ref.shape
     depth = rows.shape[1]
     times = depth // reps
-    weighted[...] = (rows[...].astype(F32) * eig_ref[...] / depth).astype(BF16)
     for q in range(reps):
+        at = slice(q * times, (q + 1) * times)
+        weighted[:, at] = (rows[:, at].astype(F32) * eig_ref[...] / depth).astype(BF16)
         alpha_scr[pl.ds(q, tile, stride=reps), :] = lax.dot_general(
-            rows[:, q * times : (q + 1) * times], basis_ref[...], CONTRACT_LAST, preferred_element_type=F32
+            rows[:, at], basis_ref[...], CONTRACT_LAST, preferred_element_type=F32
         )
     alpha_ref[...] = alpha_scr[...].astype(BF16).reshape(alpha_ref.shape)
     for w in range(0, sub, wide):
@@ -677,7 +700,7 @@
         in_specs=[
             pl.BlockSpec((tile, depth), lambda i: (i, 0)),
             pl.BlockSpec((blocks, sub, depth), lambda i: (0, 0, 0)),
-            pl.BlockSpec((1, depth), lambda i: (0, 0)),
+            pl.BlockSpec((1, times), lambda i: (0, 0)),
             pl.BlockSpec((time_local, times), lambda i: (0, 0)),
         ],
         out_specs=(
@@ -690,7 +713,7 @@
             pltpu.VMEM((wide // 128, tile * blocks, 128), F32),
             pltpu.VMEM((wide // 128, tile * blocks, 128), F32),
         ],
-    )(rows, columns, jnp.tile(time_eig, reps)[None, :], time_basis)
+    )(rows, columns, time_eig[None, :], time_basis)
 
 
 def per_device(series, space_basis, time_basis, space_eig, time_eig):

time: 230 us -> 221 us (0.961)
  Pallas kernels: 224 us -> 216 us
    pallas_call x1, Pallas kernels: 195 us -> 187 us  [solve_field(): pl.pallas_call(functools.partial(field_kernel, space_count, time_count),...]
    unnamed x3 -> x1, local copies, waits for them, and re-layouts: 4.94 us -> 3.66 us
where the time goes in v3:
time: 221 us
  Pallas kernels  216 us (98%)
  local copies, waits for them, and re-layouts  3.66 us (2%)
    pallas_call x1, Pallas kernels, solve_field(): pl.pallas_call(functools.partial(field_kernel, space_count, time_count),...  187 us
    pallas_call x1, Pallas kernels, grad_and_alpha(): pl.pallas_call(functools.partial(grad_kernel, reps, wide), out_shape=(jax...  29.6 us

profile of v3, /device:TPU:0, one launch (start us, length us, event | category | flops | bytes accessed | tf_op | source)
XLA Modules:
  0.0 220.5 jit_solution(9004250041592283673)
XLA Ops:
  0.6 3.7 %copy.7 = bf16[2048,2,128]{0,2,1:T(8,128)(2,1)} copy(bf16[2048,2,128]{2,1,0:T(2,128)(2,1)} %param.5) | data formatting | bytes 2097152 | tf_op args[0]
  4.3 186.6 %shard_map.68 = (bf16[8,256,1024]{2,1,0:T(8,128)(2,1)}, bf16[8,2,256,1024]{3,2,1,0:T(8,128)(2,1)}) custom-call(bf16[2,128,2048]{2,1,0:T(8,128)(2,1)} %bitcast.6, bf16[2048,4096]{1,0:T(8,128)(2,1)} %basis_hbm.1, bf16[128,512]{1,0:T(8,128)(2,1)} %basis_ref.1, f32[1,512]{1,0:T(1,128)} %bitcast.9, f32[1,16384]{1,0:T(1,128)} %bitcast.8), custom_call_target="tpu_custom_call" | custom-call | tf_op jit(solution)/shard_map/pallas_call | solution.py:612
  190.9 29.6 %shard_map.69 = (bf16[2048,2,128]{2,1,0:T(2,128)(2,1)}, bf16[2048,8,512]{2,1,0:T(8,128)(2,1)}) custom-call(bf16[2048,1024]{1,0:T(8,128)(2,1)} %bitcast.7, bf16[8,512,1024]{2,1,0:T(8,128)(2,1)} %bitcast.5, f32[1,512]{1,0:T(1,128)} %bitcast.10, bf16[128,512]{1,0:T(8,128)(2,1)} %basis_ref.1), custom_call_target="tpu_custom_call" | custom-call | tf_op jit(solution)/shard_map/pallas_call | solution.py:693

commit v4 on v3

--- a/solution.py
+++ b/solution.py
@@ -97,8 +97,8 @@
     pl.semaphore_wait(barrier, pairs + jnp.minimum(z, 1) + jnp.minimum(last - z, 1))
 
     def x_copy(q, j, way, step, p):
-        size = series.shape[3] // PARTS
-        at = series.at[q, j, :, pl.ds(p * size, size)]
+        size = time_local // PARTS
+        at = series.at[q, j, pl.ds(p * size, size)]
         return rcopy(at, at, xs_sem.at[q, way, step, p], xr_sem.at[q, j, p], tm=z + 1 - 2 * way)
 
     def t_copy(j, way, step, p):
@@ -189,32 +189,34 @@
         return jnp.dot(series[q, j], basis[:, at], preferred_element_type=F32)
 
     def spectral(q, j, send=True):
-        @pl.loop(0, pairs)
+        @pl.loop(0, pairs + 2)
         def _(n):
-            d = pairs - 1 - n
-            if q > 0:
-                pair_copy(q - 1, j, d).wait_send()
-            pair_out[d, j] = spectrum(q, j, 2 * chip_at(d) + 1 - core).astype(BF16)
-            pair_copy(q, j, d).start()
-
-        @pl.loop(0, pairs)
-        def _(n):
-            d = pairs - 1 - n
-            value = spectrum(q, j, peer(d))
-            pair_copy(q, j, d).wait_recv()
-            value = value + pair_in[q, d, j].astype(F32)
-
-            @pl.when(d > 0)
-            def _():
+            @pl.when(n < pairs)
+            def _():
+                d = pairs - 1 - n
                 if q > 0:
-                    chip_copy(q - 1, j, d).wait_send()
-                chip_out[d - 1, j] = value.astype(BF16)
-                if send:
-                    chip_copy(q, j, d).start()
-
-            @pl.when(d == 0)
-            def _():
-                mine[q, j] = value
+                    pair_copy(q - 1, j, d).wait_send()
+                pair_out[d, j] = spectrum(q, j, 2 * chip_at(d) + 1 - core).astype(BF16)
+                pair_copy(q, j, d).start()
+
+            @pl.when(n >= 2)
+            def _():
+                d = pairs + 1 - n
+                value = spectrum(q, j, peer(d))
+                pair_copy(q, j, d).wait_recv()
+                value = value + pair_in[q, d, j].astype(F32)
+
+                @pl.when(d > 0)
+                def _():
+                    if q > 0:
+                        chip_copy(q - 1, j, d).wait_send()
+                    chip_out[d - 1, j] = value.astype(BF16)
+                    if send:
+                        chip_copy(q, j, d).start()
+
+                @pl.when(d == 0)
+                def _():
+                    mine[q, j] = value
 
     def spectral_side(q, k, side):
         j = jnp.where(2 * z < time_count, z + k * (1 - 2 * side), z + k * (2 * side - 1))
@@ -477,13 +479,13 @@
         for p in range(PARTS):
             if work and k > 1:
                 work.pop(0)()
+            if p == 0 and k == max(1, time_count - 1):
+                for q in range(1, reps):
+                    line_start(x_of(q))
             line_part(x_of(0), k, p)
             if p == PARTS - 1:
                 line_step(t_line, k)
                 t_share_step(k)
-                if k == max(1, time_count - 2):
-                    for q in range(1, reps):
-                        line_start(x_of(q))
             if work and k == 1:
                 work.pop(0)()
         while work:
@@ -502,15 +504,34 @@
         gather_near(v)
         for h in range(1, HALVES):
             gather_start(v + h)
-        for k in range(2, time_count - 1):
-            line_step(x_of(q + 1), k)
-            spectral_step(q + 1, k, False)
+
+        @pl.when((z > 0) & (z < last))
+        def _():
+            for k in range(2, time_count - 1):
+                line_step(x_of(q + 1), k)
+                spectral_step(q + 1, k, False)
+
         gather_far(v)
 
     after = {}
 
     def then(n, act, *args):
         after.setdefault(n, []).append(functools.partial(act, *args))
+
+    def slices_flush(q):
+        spectral_flush(q, 1)
+
+        @pl.when((z > 0) & (z < last))
+        def _():
+            for k in range(2, time_count - 1):
+                spectral_flush(q, k)
+
+    def slices_of_ends(q):
+        @pl.when((z == 0) | (z == last))
+        def _():
+            for k in range(2, time_count - 1):
+                line_step(x_of(q), k)
+                spectral_step(q, k)
 
     def columns_bulk(v):
         @pl.loop(0, PIECES)
@@ -522,8 +543,8 @@
         first = q * HALVES * blocks
         if q + 1 < reps:
             then(first + blocks - 5 * unit, gather_near, q * HALVES + 1)
-            for k in range(1, time_count - 1):
-                then(first + blocks - 5 * unit, spectral_flush, q + 1, k)
+            then(first + blocks - 5 * unit, slices_flush, q + 1)
+            then(first + blocks - 4 * unit, slices_of_ends, q + 1)
             for k in range(max(2, time_count - 1), time_count):
                 then(first + blocks - 2 * unit, line_step, x_of(q + 1), k)
                 then(first + blocks - 2 * unit, spectral_step, q + 1, k)

time: 221 us -> 218 us (0.986)
  Pallas kernels: 216 us -> 213 us
    pallas_call x1, Pallas kernels: 187 us -> 184 us  [solve_field(): pl.pallas_call(functools.partial(field_kernel, space_count, time_count),...]
where the time goes in v4:
time: 218 us
  Pallas kernels  213 us (98%)
  local copies, waits for them, and re-layouts  3.66 us (2%)
    pallas_call x1, Pallas kernels, solve_field(): pl.pallas_call(functools.partial(field_kernel, space_count, time_count),...  184 us
    pallas_call x1, Pallas kernels, grad_and_alpha(): pl.pallas_call(functools.partial(grad_kernel, reps, wide), out_shape=(jax...  29.6 us

profile of v4, /device:TPU:0, one launch (start us, length us, event | category | flops | bytes accessed | tf_op | source)
XLA Modules:
  0.0 217.5 jit_solution(5649452763908031090)
XLA Ops:
  0.6 3.7 %copy.7 = bf16[2048,2,128]{0,2,1:T(8,128)(2,1)} copy(bf16[2048,2,128]{2,1,0:T(2,128)(2,1)} %param.5) | data formatting | bytes 2097152 | tf_op args[0]
  4.3 183.6 %shard_map.68 = (bf16[8,256,1024]{2,1,0:T(8,128)(2,1)}, bf16[8,2,256,1024]{3,2,1,0:T(8,128)(2,1)}) custom-call(bf16[2,128,2048]{2,1,0:T(8,128)(2,1)} %bitcast.6, bf16[2048,4096]{1,0:T(8,128)(2,1)} %basis_hbm.1, bf16[128,512]{1,0:T(8,128)(2,1)} %basis_ref.1, f32[1,512]{1,0:T(1,128)} %bitcast.9, f32[1,16384]{1,0:T(1,128)} %bitcast.8), custom_call_target="tpu_custom_call" | custom-call | tf_op jit(solution)/shard_map/pallas_call | solution.py:633
  187.9 29.6 %shard_map.69 = (bf16[2048,2,128]{2,1,0:T(2,128)(2,1)}, bf16[2048,8,512]{2,1,0:T(8,128)(2,1)}) custom-call(bf16[2048,1024]{1,0:T(8,128)(2,1)} %bitcast.7, bf16[8,512,1024]{2,1,0:T(8,128)(2,1)} %bitcast.5, f32[1,512]{1,0:T(1,128)} %bitcast.10, bf16[128,512]{1,0:T(8,128)(2,1)} %basis_ref.1), custom_call_target="tpu_custom_call" | custom-call | tf_op jit(solution)/shard_map/pallas_call | solution.py:714

commit v5 on v4

--- a/solution.py
+++ b/solution.py
@@ -565,6 +565,31 @@
     for v in range(streams - 1):
         then(total - 1 if v < streams - 2 else total + LAG * last - 2 * unit, columns_relay, v)
 
+    def lines_drain():
+        for q in range(reps):
+            line_drain(x_of(q))
+        line_drain(t_line)
+        t_share_each(lambda copy: copy.wait_send())
+
+        @pl.loop(0, time_count)
+        def _(j):
+            for d in range(pairs):
+                pair_copy(reps - 1, j, d).wait_send()
+                if d > 0:
+                    chip_copy(reps - 1, j, d).wait_send()
+
+    def rows_drain(begin, end):
+        @pl.loop(begin, end)
+        def _(n):
+            row_copy(lax.div(n, blocks), lax.rem(n, blocks)).wait()
+
+    then(total, lines_drain)
+    for v in range(streams):
+        then(total + 1, gather_drain, v)
+    then(total + 1, rows_drain, 0, (streams - 1) * blocks)
+    for v in range(streams - 2):
+        then(min(total + 2, total + LAG * last - 1), columns_finish, v)
+
     @pl.loop(0, total + LAG * last)
     def _(n):
         v = lax.div(n, blocks)
@@ -587,23 +612,9 @@
                     act()
 
     columns_relay(streams - 1)
-    for v in range(streams):
+    for v in range(max(streams - 2, 0), streams):
         columns_finish(v)
-        gather_drain(v)
-    for q in range(reps):
-        line_drain(x_of(q))
-    line_drain(t_line)
-    t_share_each(lambda copy: copy.wait_send())
-    @pl.loop(0, time_count)
-    def _(j):
-        for d in range(pairs):
-            pair_copy(reps - 1, j, d).wait_send()
-            if d > 0:
-                chip_copy(reps - 1, j, d).wait_send()
-
-    @pl.loop(0, total)
-    def _(n):
-        row_copy(lax.div(n, blocks), lax.rem(n, blocks)).wait()
+    rows_drain((streams - 1) * blocks, total)
 
     for n in range(total - min(RING, total), total):
         q, m = n // blocks, n % blocks

time: 218 us -> 217 us (level)
  no operation moved by 1% of the time
where the time goes in v5:
time: 217 us
  Pallas kernels  213 us (98%)
  local copies, waits for them, and re-layouts  3.66 us (2%)
    pallas_call x1, Pallas kernels, solve_field(): pl.pallas_call(functools.partial(field_kernel, space_count, time_count),...  183 us
    pallas_call x1, Pallas kernels, grad_and_alpha(): pl.pallas_call(functools.partial(grad_kernel, reps, wide), out_shape=(jax...  29.6 us

profile of v5, /device:TPU:0, one launch (start us, length us, event | category | flops | bytes accessed | tf_op | source)
XLA Modules:
  0.0 217.2 jit_solution(6234572624094349878)
XLA Ops:
  0.6 3.7 %copy.7 = bf16[2048,2,128]{0,2,1:T(8,128)(2,1)} copy(bf16[2048,2,128]{2,1,0:T(2,128)(2,1)} %param.5) | data formatting | bytes 2097152 | tf_op args[0]
  4.3 183.3 %shard_map.68 = (bf16[8,256,1024]{2,1,0:T(8,128)(2,1)}, bf16[8,2,256,1024]{3,2,1,0:T(8,128)(2,1)}) custom-call(bf16[2,128,2048]{2,1,0:T(8,128)(2,1)} %bitcast.6, bf16[2048,4096]{1,0:T(8,128)(2,1)} %basis_hbm.1, bf16[128,512]{1,0:T(8,128)(2,1)} %basis_ref.1, f32[1,512]{1,0:T(1,128)} %bitcast.9, f32[1,16384]{1,0:T(1,128)} %bitcast.8), custom_call_target="tpu_custom_call" | custom-call | tf_op jit(solution)/shard_map/pallas_call | solution.py:644
  187.6 29.6 %shard_map.69 = (bf16[2048,2,128]{2,1,0:T(2,128)(2,1)}, bf16[2048,8,512]{2,1,0:T(8,128)(2,1)}) custom-call(bf16[2048,1024]{1,0:T(8,128)(2,1)} %bitcast.7, bf16[8,512,1024]{2,1,0:T(8,128)(2,1)} %bitcast.5, f32[1,512]{1,0:T(1,128)} %bitcast.10, bf16[128,512]{1,0:T(8,128)(2,1)} %basis_ref.1), custom_call_target="tpu_custom_call" | custom-call | tf_op jit(solution)/shard_map/pallas_call | solution.py:725
